TPU v7x, 32 devices: a whole 2x2x4 slice. The times are simulated.
32 devices in a mesh: dp: 16 (over z, y, x), tensor: 2 (over core).
Axes of the slice: x: 2, y: 2, z: 4, core: 2. Of those that a mesh axis runs over, the one named last changes fastest.
Arguments:
- text: bfloat16 [15360, 768], P(('dp', 'tensor')), may hold values from -6 to 6
- patches: bfloat16 [192, 145, 1024], P('dp', None, 'tensor'), may hold values from -6 to 6
- segment_ids: int32 [384, 40], P('dp'), may hold values from 0 to 3, never falling along the last dimension, each value on 1 to 20 neighbouring positions
- image_of_row: int32 [384], P('dp'), may hold values from 0 to 11
- gains: bfloat16 [3, 768], replicated, may hold values from 0.25 to 1.75
- shifts: bfloat16 [3, 768], replicated, may hold values from -1.5 to 1.5
- self_qkv: bfloat16 [768, 3, 768], P(None, None, 'tensor'), may hold values from -0.21875 to 0.21875
- in_bias: bfloat16 [4, 768], P(None, 'tensor'), may hold values from -1 to 1
- self_out: bfloat16 [768, 768], P('tensor'), may hold values from -0.625 to 0.625
- cross_q: bfloat16 [768, 768], P(None, 'tensor'), may hold values from -0.21875 to 0.21875
- cross_kv: bfloat16 [1024, 2, 768], P(None, None, 'tensor'), may hold values from -0.1875 to 0.1875
- cross_out: bfloat16 [768, 768], P('tensor'), may hold values from -1.75 to 1.75
- ffn_in: bfloat16 [768, 3072], P(None, 'tensor'), may hold values from -0.21875 to 0.21875
- ffn_in_bias: bfloat16 [3072], P('tensor'), may hold values from -2.5 to 2.5
- ffn_out: bfloat16 [3072, 768], P('tensor'), may hold values from -0.109375 to 0.109375
- out_bias: bfloat16 [3, 768], replicated, may hold values from -1.5 to 1.5
- cotangent: bfloat16 [15360, 768], P(('dp', 'tensor')), may hold values from -6 to 6
Outputs:
- layer_out: float32 [15360, 768], P(('dp', 'tensor'))
- text_grad: float32 [15360, 768], P(('dp', 'tensor'))
- patch_grad: float32 [192, 145, 1024], P('dp', None, 'tensor')
- gains_grad: float32 [3, 768], replicated
- shifts_grad: float32 [3, 768], replicated
- self_qkv_grad: float32 [768, 3, 768], P(None, None, 'tensor')
- in_bias_grad: float32 [4, 768], P(None, 'tensor')
- self_out_grad: float32 [768, 768], P('tensor')
- cross_q_grad: float32 [768, 768], P(None, 'tensor')
- cross_kv_grad: float32 [1024, 2, 768], P(None, None, 'tensor')
- cross_out_grad: float32 [768, 768], P('tensor')
- ffn_in_grad: float32 [768, 3072], P(None, 'tensor')
- ffn_in_bias_grad: float32 [3072], P('tensor')
- ffn_out_grad: float32 [3072, 768], P('tensor')
- out_bias_grad: float32 [3, 768], replicated
All inputs are finite; a program needn't handle non-finite values.
Results may differ from a plain program's by a relative error of at most 0.018.
Values may be sent and summed in bfloat16 or wider, within the bound.
No kernel may reach another device: no remote copies, remote signals or barrier semaphores. Data moves between devices by JAX's collectives and lax.ppermute only.
A program may use at most 192 MiB of HBM per device.

v0:
```python
from functools import partial

import jax
import jax.numpy as jnp
from jax import lax
from jax.sharding import PartitionSpec as P

HEAD = 64


EPSILON = 1e-06
SCORE_SCALE = 0.125
NEGATIVE = -1000000000.0


def norm_rows(values, gain_row, shift_row):
    centre = values - jnp.mean(values, axis=-1, keepdims=True)
    spread = jnp.mean(centre * centre, axis=-1, keepdims=True)
    return centre * lax.rsqrt(spread + EPSILON) * gain_row + shift_row


def softmax_rows(scores):
    top = jnp.max(scores, axis=-1, keepdims=True)
    shifted = jnp.exp(scores - top)
    total = jnp.sum(shifted, axis=-1, keepdims=True)
    return (shifted / total, top + jnp.log(total))


def contract_first(left, right):
    return lax.dot_general(
        left, right, (((0,), (0,)), ((), ())), preferred_element_type=jnp.float32
    )


def contract_last(left, right):
    return lax.dot_general(
        left, right, (((1,), (1,)), ((), ())), preferred_element_type=jnp.float32
    )


def gather_rows(local_rows):
    return lax.all_gather(local_rows, "tensor", axis=0, tiled=True)


def reduce_rows(left, right, axis_right):
    rows_here = left.shape[0] // lax.axis_size("tensor")
    piece = lax.slice_in_dim(left, 0, rows_here * lax.axis_size("tensor"), axis=0)
    return lax.psum_scatter(
        lax.dot_general(
            piece, right, (((1,), (axis_right,)), ((), ())), preferred_element_type=jnp.float32
        ),
        "tensor",
        scatter_dimension=0,
        tiled=True,
    )


def attend(queries, keys, values, same):
    scores = (
        jnp.einsum("rqhe,rkhe->rhqk", queries, keys, preferred_element_type=jnp.float32)
        * SCORE_SCALE
    )
    if same is not None:
        scores = jnp.where(same, scores, NEGATIVE)
    probs, lse = softmax_rows(scores)
    mixed = jnp.einsum(
        "rhqk,rkhe->rqhe", probs.astype(jnp.bfloat16), values, preferred_element_type=jnp.float32
    )
    return (mixed.reshape(-1, mixed.shape[2] * mixed.shape[3]).astype(jnp.bfloat16), lse)


def attention_back(queries, keys, values, lse, out_grad, same):
    scores = (
        jnp.einsum("rqhe,rkhe->rhqk", queries, keys, preferred_element_type=jnp.float32)
        * SCORE_SCALE
    )
    if same is not None:
        scores = jnp.where(same, scores, NEGATIVE)
    probs = jnp.exp(scores - lse)
    values_grad = jnp.einsum(
        "rhqk,rqhe->rkhe", probs.astype(jnp.bfloat16), out_grad, preferred_element_type=jnp.float32
    )
    probs_grad = jnp.einsum("rqhe,rkhe->rhqk", out_grad, values, preferred_element_type=jnp.float32)
    scores_grad = (
        probs * (probs_grad - jnp.sum(probs * probs_grad, axis=-1, keepdims=True))
    ).astype(jnp.bfloat16)
    queries_grad = (
        jnp.einsum("rhqk,rkhe->rqhe", scores_grad, keys, preferred_element_type=jnp.float32)
        * SCORE_SCALE
    )
    keys_grad = (
        jnp.einsum("rhqk,rqhe->rkhe", scores_grad, queries, preferred_element_type=jnp.float32)
        * SCORE_SCALE
    )
    return (queries_grad, keys_grad, values_grad)


def forward_pass(text, patches, segment_ids, image_of_row, weights):
    (
        gains,
        shifts,
        self_qkv,
        in_bias,
        self_out,
        cross_q,
        cross_kv,
        cross_out,
        ffn_in,
        ffn_in_bias,
        ffn_out,
        out_bias,
    ) = weights
    rows_count, length = segment_ids.shape
    image_count, patch_count = (patches.shape[0], patches.shape[1])
    width = text.shape[1]
    local_width = self_out.shape[0]
    heads_here = local_width // HEAD
    quad = (rows_count, length, heads_here, HEAD)
    patch_quad = (rows_count, patch_count, heads_here, HEAD)
    gain_rows = gains.astype(jnp.float32)
    shift_rows = shifts.astype(jnp.float32)
    bias_in = in_bias.astype(jnp.float32)
    bias_out = out_bias.astype(jnp.float32)
    kept = {}
    resid = text.astype(jnp.float32)
    kept["resid_zero"] = resid
    full_one = gather_rows(norm_rows(resid, gain_rows[0], shift_rows[0]).astype(jnp.bfloat16))
    project = jnp.dot(
        full_one, self_qkv.reshape(width, 3 * local_width), preferred_element_type=jnp.float32
    ).reshape(-1, 3, local_width)
    queries = (project[:, 0] + bias_in[0]).astype(jnp.bfloat16).reshape(quad)
    keys_self = project[:, 1].astype(jnp.bfloat16).reshape(quad)
    values_self = (project[:, 2] + bias_in[1]).astype(jnp.bfloat16).reshape(quad)
    same = (segment_ids[:, :, None] == segment_ids[:, None, :])[:, None]
    attended_self, lse_self = attend(queries, keys_self, values_self, same)
    resid = resid + reduce_rows(attended_self, self_out, 0) + bias_out[0]
    kept.update(
        full_one=full_one,
        queries=queries,
        keys_self=keys_self,
        values_self=values_self,
        same=same,
        lse_self=lse_self,
        attended_self=attended_self,
        resid_one=resid,
    )
    full_two = gather_rows(norm_rows(resid, gain_rows[1], shift_rows[1]).astype(jnp.bfloat16))
    cross_queries = (
        (jnp.dot(full_two, cross_q, preferred_element_type=jnp.float32) + bias_in[2])
        .astype(jnp.bfloat16)
        .reshape(quad)
    )
    empty = jnp.zeros((image_count * patch_count, 2 * local_width), jnp.float32)
    piece = jax.tree.map(lambda part: lax.all_gather(part, "tensor", axis=2, tiled=True), patches)
    count = piece.shape[2]
    rows = lax.slice_in_dim(cross_kv, 0, count, axis=0).reshape(count, 2 * local_width)
    patch_proj = empty + jnp.dot(piece.reshape(-1, count), rows, preferred_element_type=jnp.float32)
    patch_proj = patch_proj.reshape(image_count, patch_count, 2, local_width)
    patch_keys = patch_proj[:, :, 0].astype(jnp.bfloat16)
    patch_values = (patch_proj[:, :, 1] + bias_in[3]).astype(jnp.bfloat16)
    pick = (image_of_row[:, None] == lax.iota(jnp.int32, image_count)[None, :]).astype(jnp.bfloat16)
    row_keys = (
        jnp.einsum("ri,ipe->rpe", pick, patch_keys, preferred_element_type=jnp.float32)
        .astype(jnp.bfloat16)
        .reshape(patch_quad)
    )
    row_values = (
        jnp.einsum("ri,ipe->rpe", pick, patch_values, preferred_element_type=jnp.float32)
        .astype(jnp.bfloat16)
        .reshape(patch_quad)
    )
    attended_cross, lse_cross = attend(cross_queries, row_keys, row_values, None)
    resid = resid + reduce_rows(attended_cross, cross_out, 0) + bias_out[1]
    kept.update(
        full_two=full_two,
        cross_queries=cross_queries,
        row_keys=row_keys,
        row_values=row_values,
        pick=pick,
        lse_cross=lse_cross,
        attended_cross=attended_cross,
        resid_two=resid,
    )
    full_three = gather_rows(norm_rows(resid, gain_rows[2], shift_rows[2]).astype(jnp.bfloat16))
    inner = jnp.dot(full_three, ffn_in, preferred_element_type=jnp.float32) + ffn_in_bias.astype(
        jnp.float32
    )
    hidden = jax.nn.gelu(inner, approximate=False).astype(jnp.bfloat16)
    result = resid + reduce_rows(hidden, ffn_out, 0) + bias_out[2]
    kept.update(full_three=full_three, inner=inner, hidden=hidden)
    return (result, kept)


def local(
    text,
    patches,
    segment_ids,
    image_of_row,
    gains,
    shifts,
    self_qkv,
    in_bias,
    self_out,
    cross_q,
    cross_kv,
    cross_out,
    ffn_in,
    ffn_in_bias,
    ffn_out,
    out_bias,
    cotangent,
):
    weights = (
        gains,
        shifts,
        self_qkv,
        in_bias,
        self_out,
        cross_q,
        cross_kv,
        cross_out,
        ffn_in,
        ffn_in_bias,
        ffn_out,
        out_bias,
    )
    result, kept = forward_pass(text, patches, segment_ids, image_of_row, weights)
    text_again, patches_again, _ = lax.optimization_barrier((text, patches, result))
    _, kept = forward_pass(text_again, patches_again, segment_ids, image_of_row, weights)
    width = text.shape[1]
    local_width = self_out.shape[0]
    kv_width = cross_kv.shape[0]
    image_count, patch_count = (patches.shape[0], patches.shape[1])
    rows_count = segment_ids.shape[0]
    gain_rows = gains.astype(jnp.float32)
    shift_rows = shifts.astype(jnp.float32)
    grad = cotangent.astype(jnp.float32)
    bias_three = jnp.sum(grad, axis=0)
    grad_full = gather_rows(grad.astype(jnp.bfloat16))
    ffn_out_grad = contract_first(kept["hidden"], grad_full)
    hidden_grad = contract_last(grad_full, ffn_out)
    _, gelu_back = jax.vjp(partial(jax.nn.gelu, approximate=False), kept["inner"])
    inner_grad = gelu_back(hidden_grad)[0].astype(jnp.bfloat16)
    ffn_in_bias_grad = jnp.sum(inner_grad.astype(jnp.float32), axis=0)
    ffn_in_grad = contract_first(kept["full_three"], inner_grad)
    normed_grad = reduce_rows(inner_grad, ffn_in, 1)
    _, norm_back = jax.vjp(norm_rows, kept["resid_two"], gain_rows[2], shift_rows[2])
    resid_grad, gain_three, shift_three = norm_back(normed_grad)
    grad = grad + resid_grad
    bias_two = jnp.sum(grad, axis=0)
    grad_full = gather_rows(grad.astype(jnp.bfloat16))
    cross_out_grad = contract_first(kept["attended_cross"], grad_full)
    attended_grad = contract_last(grad_full, cross_out).astype(jnp.bfloat16)
    query_grad, key_grad, value_grad = attention_back(
        kept["cross_queries"],
        kept["row_keys"],
        kept["row_values"],
        kept["lse_cross"],
        attended_grad.reshape(kept["cross_queries"].shape),
        None,
    )
    pick_float = kept["pick"].astype(jnp.float32)
    image_keys_grad = jnp.einsum(
        "ri,rpe->ipe",
        pick_float,
        key_grad.reshape(rows_count, patch_count, local_width),
        preferred_element_type=jnp.float32,
    ).astype(jnp.bfloat16)
    image_values_grad = jnp.einsum(
        "ri,rpe->ipe",
        pick_float,
        value_grad.reshape(rows_count, patch_count, local_width),
        preferred_element_type=jnp.float32,
    ).astype(jnp.bfloat16)
    cross_query_grad = query_grad.reshape(-1, local_width).astype(jnp.bfloat16)
    cross_q_bias = jnp.sum(cross_query_grad.astype(jnp.float32), axis=0)
    cross_v_bias = jnp.sum(image_values_grad.astype(jnp.float32), axis=(0, 1))
    cross_q_grad = contract_first(kept["full_two"], cross_query_grad)
    kv_grad_flat = jnp.stack([image_keys_grad, image_values_grad], axis=2).reshape(
        image_count * patch_count, 2 * local_width
    )
    piece = lax.all_gather(patches, "tensor", axis=2, tiled=True)
    cross_kv_grad = contract_first(piece.reshape(-1, piece.shape[2]), kv_grad_flat).reshape(
        kv_width, 2, local_width
    )
    patch_terms = contract_last(kv_grad_flat, cross_kv.reshape(kv_width, 2 * local_width)).reshape(
        image_count, patch_count, kv_width
    )
    patch_grad = lax.psum_scatter(
        patch_terms.astype(jnp.bfloat16), "tensor", scatter_dimension=2, tiled=True
    ).astype(jnp.float32)
    normed_grad = reduce_rows(cross_query_grad, cross_q, 1)
    _, norm_back = jax.vjp(norm_rows, kept["resid_one"], gain_rows[1], shift_rows[1])
    resid_grad, gain_two, shift_two = norm_back(normed_grad)
    grad = grad + resid_grad
    bias_one = jnp.sum(grad, axis=0)
    grad_full = gather_rows(grad.astype(jnp.bfloat16))
    self_out_grad = contract_first(kept["attended_self"], grad_full)
    attended_grad = contract_last(grad_full, self_out).astype(jnp.bfloat16)
    query_grad, key_grad, value_grad = attention_back(
        kept["queries"],
        kept["keys_self"],
        kept["values_self"],
        kept["lse_self"],
        attended_grad.reshape(kept["queries"].shape),
        kept["same"],
    )
    query_low = query_grad.reshape(-1, local_width).astype(jnp.bfloat16)
    key_low = key_grad.reshape(-1, local_width).astype(jnp.bfloat16)
    value_low = value_grad.reshape(-1, local_width).astype(jnp.bfloat16)
    stacked = jnp.stack([query_low, key_low, value_low], axis=1).reshape(-1, 3 * local_width)
    self_qkv_grad = contract_first(kept["full_one"], stacked).reshape(width, 3, local_width)
    in_bias_grad = jnp.stack(
        [
            jnp.sum(query_low.astype(jnp.float32), axis=0),
            jnp.sum(value_low.astype(jnp.float32), axis=0),
            cross_q_bias,
            cross_v_bias,
        ]
    )
    normed_grad = reduce_rows(stacked, self_qkv.reshape(width, 3 * local_width), 1)
    _, norm_back = jax.vjp(norm_rows, kept["resid_zero"], gain_rows[0], shift_rows[0])
    resid_grad, gain_one, shift_one = norm_back(normed_grad)
    text_grad = grad + resid_grad
    gains_grad, shifts_grad, out_bias_grad = lax.psum(
        (
            jnp.stack([gain_one, gain_two, gain_three]),
            jnp.stack([shift_one, shift_two, shift_three]),
            jnp.stack([bias_one, bias_two, bias_three]),
        ),
        ("dp", "tensor"),
    )
    (
        self_qkv_grad,
        in_bias_grad,
        self_out_grad,
        cross_q_grad,
        cross_kv_grad,
        cross_out_grad,
        ffn_in_grad,
        ffn_in_bias_grad,
        ffn_out_grad,
    ) = lax.psum(
        (
            self_qkv_grad,
            in_bias_grad,
            self_out_grad,
            cross_q_grad,
            cross_kv_grad,
            cross_out_grad,
            ffn_in_grad,
            ffn_in_bias_grad,
            ffn_out_grad,
        ),
        "dp",
    )
    return (
        result,
        text_grad,
        patch_grad,
        gains_grad,
        shifts_grad,
        self_qkv_grad,
        in_bias_grad,
        self_out_grad,
        cross_q_grad,
        cross_kv_grad,
        cross_out_grad,
        ffn_in_grad,
        ffn_in_bias_grad,
        ffn_out_grad,
        out_bias_grad,
    )


def solution(mesh):
    in_specs = (
        P(("dp", "tensor"), None),
        P("dp", None, "tensor"),
        P("dp", None),
        P("dp"),
        P(),
        P(),
        P(None, None, "tensor"),
        P(None, "tensor"),
        P("tensor", None),
        P(None, "tensor"),
        P(None, None, "tensor"),
        P("tensor", None),
        P(None, "tensor"),
        P("tensor"),
        P("tensor", None),
        P(),
        P(("dp", "tensor"), None),
    )
    out_specs = (
        P(("dp", "tensor"), None),
        P(("dp", "tensor"), None),
        P("dp", None, "tensor"),
        P(),
        P(),
        P(None, None, "tensor"),
        P(None, "tensor"),
        P("tensor", None),
        P(None, "tensor"),
        P(None, None, "tensor"),
        P("tensor", None),
        P(None, "tensor"),
        P("tensor"),
        P("tensor", None),
        P(),
    )
    return jax.shard_map(local, mesh=mesh, in_specs=in_specs, out_specs=out_specs, check_vma=False)
```

profile of v0, /device:TPU:0, one launch (start us, length us, event | category | flops | bytes accessed | tf_op | source)
XLA Modules:
  0.0 1174.5 jit_solution(8375168360843895289)
XLA Ops:
  18.3 8.2 all-gather.12.cloned.1.call-done
  74.8 12.0 %all-gather.14.cloned.1.call-done = bf16[12,145,1024]{2,1,0:T(8,128)(2,1)} async-done(((bf16[12,145,512]{2,1,0:T(8,128)(2,1)}), bf16[12,145,1024]{2,1,0:T(8,128)(2,1)}) %all-gather.14.cloned.1.call-update) | async-done | bytes 3563536 | tf_op jit(solution)/shard_map/all_gather | solution.py:154
  127.3 25.0 %fusion.187 = (f32[24,6,40]{2,1,0:T(8,128)S(1)}, f32[24,6,40,145]{3,2,1,0:T(8,128)S(1)}) fusion(f32[24,6,40,145]{3,2,1,0:T(8,128)S(1)} %fusion.83), kind=kOutput, calls=%fused_computation.316 | output fusion | flops 3340944 | bytes 6704640 | tf_op jit(solution)/shard_map/sub | solution.py:24
  165.6 12.2 %reduce-scatter.12.cloned.1.call-done = f32[480,768]{1,0:T(8,128)} async-done(((f32[960,768]{1,0:T(8,128)}), f32[480,768]{1,0:T(8,128)}) %reduce-scatter.12.cloned.1.call-update) | async-done | bytes 1474576 | tf_op jit(solution)/shard_map/reduce_scatter | solution.py:48
  182.2 8.8 reduce-scatter.14.cloned.1.call-start
  193.3 20.3 %fusion.51 = f32[960,768]{1,0:T(8,128)} fusion(bf16[1536,768]{1,0:T(8,128)(2,1)S(1)} %copy-done, bf16[960,768]{1,0:T(8,128)(2,1)} %all-gather.18.cloned.1.call-done, bf16[768,1536]{1,0:T(8,128)(2,1)} %param.29, f32[1536]{0:T(1024)S(1)} %convert_element_type.311), kind=kOutput, calls=%fused_computation.118 | convolution fusion | flops 4627169280 | bytes 9148416 | tf_op jit(solution)/shard_map/dot_general | solution.py:49
  213.7 12.2 %reduce-scatter.14.cloned.1.call-done = f32[480,768]{1,0:T(8,128)} async-done(((f32[960,768]{1,0:T(8,128)}), f32[480,768]{1,0:T(8,128)}) %reduce-scatter.14.cloned.1.call-update) | async-done | bytes 1474576 | tf_op jit(solution)/shard_map/reduce_scatter | solution.py:48
  230.8 11.0 all-gather.20.cloned.1.call-done
  282.4 11.6 reduce-scatter.16.cloned.1.call-done
  298.1 11.5 all-gather.22.cloned.1.call-done
  320.4 7.1 copy.86
  331.9 7.1 copy.88
  364.1 11.9 %reduce-scatter.18.cloned.1.call-done = f32[480,768]{1,0:T(8,128)} async-done(((f32[960,768]{1,0:T(8,128)}), f32[480,768]{1,0:T(8,128)}) %reduce-scatter.18.cloned.1.call-update) | async-done | bytes 1474576 | tf_op jit(solution)/shard_map/reduce_scatter | solution.py:48
  381.0 10.5 all-gather.26.cloned.1.call-done
  391.5 7.0 fusion.193
  403.8 19.0 %convert_reduce_fusion = (f32[1536]{0:T(1024)S(1)}, bf16[960,1536]{1,0:T(8,128)(2,1)S(1)}, f32[960,1536]{1,0:T(8,128)}) fusion(f32[960,1536]{1,0:T(8,128)} %fusion.193, f32[1536]{0:T(1024)S(1)} %convert_element_type.311, bf16[960,768]{1,0:T(8,128)(2,1)} %all-gather.28.cloned.1.call-done, bf16[1536,768]{1,0:T(8,128)(2,1)S(1)} %copy-done), kind=kOutput, calls=%fused_computation.10 | convolution fusion | flops 2375514624 | bytes 18591744 | tf_op jit(solution)/shard_map/dot_general | solution.py:36
  428.4 12.2 %reduce-scatter.20.cloned.1.call-done = f32[480,768]{1,0:T(8,128)} async-done(((f32[960,768]{1,0:T(8,128)}), f32[480,768]{1,0:T(8,128)}) %reduce-scatter.20.cloned.1.call-update) | async-done | bytes 1474576 | tf_op jit(solution)/shard_map/reduce_scatter | solution.py:48
  446.0 10.8 all-gather.30.cloned.1.call-done
  480.5 7.6 fusion.27
  577.2 7.2 fusion.200
  584.5 10.1 fusion.29
  628.1 81.8 %all-reduce.1 = (f32[4,384]{1,0:T(4,128)}, f32[1536]{0:T(1024)}) all-reduce(f32[4,384]{1,0:T(4,128)S(1)} %pad_maximum_fusion.4, f32[1536]{0:T(1024)S(1)} %get-tuple-element.56), channel_id=1, replica_groups=mesh['dp'=16,'tensor'=2] {'dp'}, use_global_device_ids=true, to_apply=%region_50.51 | all-reduce | flops 3072 | bytes 24576 | tf_op jit(solution)/shard_map/psum | solution.py:343
  712.7 41.4 %all-reduce = (f32[3,768]{1,0:T(4,128)}, f32[3,768]{1,0:T(4,128)}, f32[3,768]{1,0:T(4,128)}) all-reduce(f32[3,768]{1,0:T(4,128)S(1)} %pad_maximum_fusion.1, f32[3,768]{1,0:T(4,128)S(1)} %pad_maximum_fusion.2, f32[3,768]{1,0:T(4,128)S(1)} %pad_maximum_fusion.3), channel_id=1, replica_groups=mesh['dp'=16,'tensor'=2] {'dp','tensor'}, use_global_device_ids=true, to_apply=%region_40.41 | all-reduce | flops 6912 | bytes 55296 | tf_op jit(solution)/shard_map/psum | solution.py:325
  757.1 392.6 %all-reduce.5.cloned.1.call-done = (f32[768,3,384]{2,0,1:T(8,128)}, f32[384,768]{1,0:T(8,128)}, f32[768,384]{1,0:T(8,128)}, f32[1024,2,384]{2,1,0:T(2,128)}, f32...) async-done(((f32[768,3,384]{2,0,1:T(8,128)}, f32[384,768]{1,0:T(8,128)}, f32[768,384]{1,0:T(8,128)}, f32[1024,2,384]{2,1,0:T(2,128)}, ...) | async-done | bytes 19660816 | tf_op jit(solution)/shard_map/psum | solution.py:343
  (402 shorter events, 399.6 us)
Async XLA Ops:
  7.2 186.1 %copy-start = (bf16[1536,768]{1,0:T(8,128)(2,1)S(1)}, bf16[1536,768]{1,0:T(8,128)(2,1)}, u32[]{:S(2)}) copy-start(bf16[1536,768]{1,0:T(8,128)(2,1)} %param.31) | copy-start | bytes 7077892
  7.2 19.3 %all-gather.12.cloned.1.call-start = ((), (), s32[]{:S(2)}) async-start(), calls=%async_computation.9 | async-start | bytes 2211840 | tf_op jit(solution)/shard_map/all_gather | solution.py:42
  11.6 217.9 %copy-start.55 = (f32[768]{0:T(1024)}, f32[768]{0:T(1024)S(1)}, u32[]{:S(2)}) copy-start(f32[768]{0:T(1024)S(1)} %get-tuple-element.96) | copy-start | bytes 9220
  14.0 56.9 %reduce-scatter.10.cloned.1.call-start = ((), (), s32[]{:S(2)}) async-start(), calls=%async_computation.10 | async-start | bytes 4423680 | tf_op jit(solution)/shard_map/reduce_scatter | solution.py:48
  58.7 28.1 %all-gather.14.cloned.1.call-start = ((), (), s32[]{:S(2)}) async-start(), calls=%async_computation.11 | async-start | bytes 5603328 | tf_op jit(solution)/shard_map/all_gather | solution.py:154
  59.4 57.0 %all-gather.16.cloned.1.call-start = ((), (), s32[]{:S(2)}) async-start(), calls=%async_computation.12 | async-start | bytes 2211840 | tf_op jit(solution)/shard_map/all_gather | solution.py:42
  74.5 103.2 %reduce-scatter.12.cloned.1.call-start = ((), (), s32[]{:S(2)}) async-start(), calls=%async_computation.13 | async-start | bytes 4423680 | tf_op jit(solution)/shard_map/reduce_scatter | solution.py:48
  165.5 27.8 %all-gather.18.cloned.1.call-start = ((), (), s32[]{:S(2)}) async-start(), calls=%async_computation.14 | async-start | bytes 2211840 | tf_op jit(solution)/shard_map/all_gather | solution.py:42
  182.2 43.7 %reduce-scatter.14.cloned.1.call-start = ((), (), s32[]{:S(2)}) async-start(), calls=%async_computation.15 | async-start | bytes 4423680 | tf_op jit(solution)/shard_map/reduce_scatter | solution.py:48
  213.6 28.2 %all-gather.20.cloned.1.call-start = ((), (), s32[]{:S(2)}) async-start(), calls=%async_computation.16 | async-start | bytes 2211840 | tf_op jit(solution)/shard_map/all_gather | solution.py:42
  230.8 63.2 %reduce-scatter.16.cloned.1.call-start = ((), (), s32[]{:S(2)}) async-start(), calls=%async_computation.17 | async-start | bytes 4423680 | tf_op jit(solution)/shard_map/reduce_scatter | solution.py:48
  281.7 27.9 %all-gather.22.cloned.1.call-start = ((), (), s32[]{:S(2)}) async-start(), calls=%async_computation.18 | async-start | bytes 5603328 | tf_op jit(solution)/shard_map/all_gather | solution.py:154
  282.3 56.7 %all-gather.24.cloned.1.call-start = ((), (), s32[]{:S(2)}) async-start(), calls=%async_computation.19 | async-start | bytes 2211840 | tf_op jit(solution)/shard_map/all_gather | solution.py:42
  297.9 78.2 %reduce-scatter.18.cloned.1.call-start = ((), (), s32[]{:S(2)}) async-start(), calls=%async_computation.20 | async-start | bytes 4423680 | tf_op jit(solution)/shard_map/reduce_scatter | solution.py:48
  363.8 27.7 %all-gather.26.cloned.1.call-start = ((), (), s32[]{:S(2)}) async-start(), calls=%async_computation.21 | async-start | bytes 2211840 | tf_op jit(solution)/shard_map/all_gather | solution.py:42
  380.4 23.4 %all-gather.28.cloned.1.call-start = ((), (), s32[]{:S(2)}) async-start(), calls=%async_computation.22 | async-start | bytes 2211840 | tf_op jit(solution)/shard_map/all_gather | solution.py:42
  381.0 59.7 %reduce-scatter.20.cloned.1.call-start = ((), (), s32[]{:S(2)}) async-start(), calls=%async_computation.23 | async-start | bytes 4423680 | tf_op jit(solution)/shard_map/reduce_scatter | solution.py:48
  428.4 28.4 %all-gather.30.cloned.1.call-start = ((), (), s32[]{:S(2)}) async-start(), calls=%async_computation.24 | async-start | bytes 2211840 | tf_op jit(solution)/shard_map/all_gather | solution.py:42
  445.7 47.0 %reduce-scatter.22.cloned.1.call-start = ((), (), s32[]{:S(2)}) async-start(), calls=%async_computation.25 | async-start | bytes 4423680 | tf_op jit(solution)/shard_map/reduce_scatter | solution.py:48
  480.5 49.1 %all-gather.32.cloned.1.call-start = ((), (), s32[]{:S(2)}) async-start(), calls=%async_computation.26 | async-start | bytes 2211840 | tf_op jit(solution)/shard_map/all_gather | solution.py:42
  497.7 126.3 %reduce-scatter.26.cloned.1.call-start = ((), (), s32[]{:S(2)}) async-start(), calls=%async_computation.28 | async-start | bytes 5603328 | tf_op jit(solution)/shard_map/reduce_scatter | solution.py:289
  528.7 181.2 %reduce-scatter.24.cloned.1.call-start = ((), (), s32[]{:S(2)}) async-start(), calls=%async_computation.27 | async-start | bytes 4423680 | tf_op jit(solution)/shard_map/reduce_scatter | solution.py:48
  572.8 577.0 %all-reduce.5.cloned.1.call-start = ((), (), s32[]{:S(2)}) async-start(), calls=%async_computation.29 | async-start | bytes 39321600 | tf_op jit(solution)/shard_map/psum | solution.py:343
  623.9 87.9 %copy-start.61 = (f32[480]{0:T(512)S(1)}, f32[480]{0:T(512)}, u32[]{:S(2)}) copy-start(f32[480]{0:T(512)} %copy-done.60) | copy-start | bytes 5764
  (78 other events, 692.7 us)
Sparse Core Ops, SparseCore 0:
  14.1 12.3 all-gather.11
  58.8 12.0 reduce-scatter.9
  72.5 14.2 all-gather.13
  88.7 10.8 all-gather.15
  165.6 12.0 reduce-scatter.11
  182.3 10.9 all-gather.17
  213.8 12.0 reduce-scatter.13
  230.9 10.9 all-gather.19
  281.8 12.0 reduce-scatter.15
  295.3 14.2 all-gather.21
  311.8 10.8 all-gather.23
  364.0 12.0 reduce-scatter.17
  380.5 10.9 all-gather.25
  392.9 10.8 all-gather.27
  428.5 12.0 reduce-scatter.19
  445.8 10.9 all-gather.29
  480.6 12.0 reduce-scatter.21
  497.8 10.9 all-gather.31
  528.8 12.9 reduce-scatter.25
  572.9 12.1 reduce-scatter.23
  623.8 525.8 all-reduce.4
where the time goes:
time: 1190 us; the launch traced here: 1170 us
  waiting for transfers between devices  537 us (45%)
  matrix products  209 us (18%)
  local copies, waits for them, and re-layouts  188 us (16%)
  blocking collectives  123 us (10%)
  other arithmetic  90.7 us (8%)
  between operations  15.9 us (1%)
    psum x1, waiting for transfers between devices, local(): lax.psum((self_qkv_grad, in_bias_grad, self_out_grad, cross_q_grad, cross...  393 us
    psum x1, blocking collectives, local(): lax.psum((self_qkv_grad, in_bias_grad, self_out_grad, cross_q_grad, cross...  81.8 us
    reduce_scatter x8, waiting for transfers between devices, reduce_rows(): lax.psum_scatter(lax.dot_general(piece, right, (((1,), (axis_right,)), ((...  70.4 us
    unnamed x175, local copies, waits for them, and re-layouts  52.7 us
    all_gather x9, waiting for transfers between devices, gather_rows(): return lax.all_gather(local_rows, 'tensor', axis=0, tiled=True)  48.1 us
    dot_general x8, matrix products, reduce_rows(): lax.dot_general(piece, right, (((1,), (axis_right,)), ((), ())), preferre...  46.7 us
    psum x1, blocking collectives, local(): lax.psum((jnp.stack([gain_one, gain_two, gain_three]), jnp.stack([shift_o...  41.4 us
    dot_general x7, matrix products, contract_first(): lax.dot_general(left, right, (((0,), (0,)), ((), ())), preferred_element_...  33.3 us
  transfers between devices with their start and end apart: 21, of which 16 were waited for; matrix products, arithmetic and copies ran while one was open for 18% of the time, Pallas kernels for 0%

commit v1 on v0

v1 whole, which is shorter than its diff:
```python
import functools

import jax
import jax.numpy as jnp
from jax import lax
from jax.experimental import pallas as pl
from jax.experimental.pallas import tpu as pltpu
from jax.sharding import PartitionSpec as P

HEAD = 64
EPSILON = 1e-06
SCALE = 0.125
NEGATIVE = -1000000000.0
F32 = jnp.float32
BF16 = jnp.bfloat16
VMEM_BYTES = 60 * 1024 * 1024


def dot_nn(a, b):
    return lax.dot_general(a, b, (((1,), (0,)), ((), ())), preferred_element_type=F32)


def dot_nt(a, b):
    return lax.dot_general(a, b, (((1,), (1,)), ((), ())), preferred_element_type=F32)


def dot_tn(a, b):
    return lax.dot_general(a, b, (((0,), (0,)), ((), ())), preferred_element_type=F32)


def norm_parts(v):
    centre = v - jnp.mean(v, axis=-1, keepdims=True)
    spread = jnp.mean(centre * centre, axis=-1, keepdims=True)
    r = lax.rsqrt(spread + EPSILON)
    return centre * r, r


def norm_back(dn, y, r, gain):
    w = dn * gain
    return r * (w - jnp.mean(w, axis=-1, keepdims=True) - y * jnp.mean(w * y, axis=-1, keepdims=True))


def spread_heads(row, heads):
    column = lax.broadcasted_iota(jnp.int32, row.shape, 1) // HEAD
    return jnp.concatenate(
        [jnp.where(column == h, row, 0.0) for h in range(heads)], axis=0
    ).astype(BF16)


def join_heads(wide, length, heads):
    column = lax.broadcasted_iota(jnp.int32, (length, heads * HEAD), 1) // HEAD
    out = wide[0:length]
    for h in range(1, heads):
        out = jnp.where(column == h, wide[h * length : (h + 1) * length], out)
    return out


def softmax_columns(st):
    top = jnp.max(st, axis=0, keepdims=True)
    e = jnp.exp(st - top)
    return e / jnp.sum(e, axis=0, keepdims=True)


def self_fwd_kernel(rows, length, heads, half, xo, xp, gains, shifts, w, bias, wo, segk, segq,
                    n1, q, k, v, p, a, part):
    i = pl.program_id(0)
    x = jnp.where(i < half, xo[...].astype(F32), xp[...].astype(F32))
    y, _ = norm_parts(x)
    n = (y * gains[0:1, :].astype(F32) + shifts[0:1, :].astype(F32)).astype(BF16)
    n1[...] = n
    b = bias[...].astype(F32)
    qv = (dot_nn(n, w[0]) + b[0:1]).astype(BF16)
    kv = dot_nn(n, w[1]).astype(BF16)
    vv = (dot_nn(n, w[2]) + b[1:2]).astype(BF16)
    q[...] = qv
    k[...] = kv
    v[...] = vv
    qf, kf, vf = qv.astype(F32), kv.astype(F32), vv.astype(F32)
    outs = []
    for r in range(rows):
        at = slice(r * length, (r + 1) * length)
        kr = kf[at].astype(BF16)
        vr = vf[at].astype(BF16)
        st = dot_nt(kr, spread_heads(qf[at], heads)) * SCALE
        st = jnp.where(segk[r] == segq[r], st, NEGATIVE)
        pr = softmax_columns(st).astype(BF16)
        p[r] = pr
        outs.append(join_heads(dot_tn(pr, vr), length, heads))
    av = jnp.concatenate(outs, axis=0).astype(BF16)
    a[...] = av
    part[...] = dot_nn(av, wo[...]).astype(BF16)


def project_kernel(place, po, pp, w0, w1, bias, kv):
    x = dot_nn(po[0], w0[...]) + dot_nn(pp[0], w1[...])
    kv[0] = (x + bias[...]).astype(BF16)


def cross_fwd_kernel(rows, length, heads, half, pick, xo, xp, part, recv, gains, shifts, bias, out_bias,
                     wq, kv, wo, h1, n2, c2, p, a, part2):
    i = pl.program_id(0)
    x = jnp.where(i < half, xo[...].astype(F32), xp[...].astype(F32))
    h = x + (part[...].astype(F32) + recv[...].astype(F32)) + out_bias[0:1, :].astype(F32)
    h1[...] = h
    y, _ = norm_parts(h)
    n = (y * gains[1:2, :].astype(F32) + shifts[1:2, :].astype(F32)).astype(BF16)
    n2[...] = n
    cv = (dot_nn(n, wq[...]) + bias[2:3, :].astype(F32)).astype(BF16)
    c2[...] = cv
    cf = cv.astype(F32)
    width = heads * HEAD
    outs = []
    for r in range(rows):
        at = slice(r * length, (r + 1) * length)
        im = pick[i * rows + r]
        kr = kv[im, :, 0:width]
        vr = kv[im, :, width : 2 * width]
        st = dot_nt(kr, spread_heads(cf[at], heads)) * SCALE
        pr = softmax_columns(st).astype(BF16)
        p[r] = pr
        outs.append(join_heads(dot_tn(pr, vr), length, heads))
    av = jnp.concatenate(outs, axis=0).astype(BF16)
    a[...] = av
    part2[...] = dot_nn(av, wo[...]).astype(BF16)


def ffn_kernel(half, chunk, h1, part, recv, eo, ep, gains, shifts, out_bias, w_in, b_in, w_out,
               h2, n3, m3, du3, e3, part_own, part_par, pdn, b_grad):
    i = pl.program_id(0)
    h = h1[...] + (part[...].astype(F32) + recv[...].astype(F32)) + out_bias[1:2, :].astype(F32)
    h2[...] = h
    y, _ = norm_parts(h)
    n = (y * gains[2:3, :].astype(F32) + shifts[2:3, :].astype(F32)).astype(BF16)
    n3[...] = n
    e = jnp.where(i < half, eo[...].astype(F32), ep[...].astype(F32)).astype(BF16)
    e3[...] = e

    @pl.when(i == 0)
    def _():
        b_grad[...] = jnp.zeros_like(b_grad)

    out_sum = None
    back_sum = None
    for c in range(w_in.shape[1] // chunk):
        at = slice(c * chunk, (c + 1) * chunk)
        u = dot_nn(n, w_in[:, at]) + b_in[:, at].astype(F32)
        cdf = 0.5 * (1.0 + lax.erf(u * 0.7071067811865476))
        m = (u * cdf).astype(BF16)
        m3[:, at] = m
        slope = cdf + u * (jnp.exp(-0.5 * u * u) * 0.3989422804014327)
        d = (dot_nt(e, w_out[at, :]) * slope).astype(BF16)
        du3[:, at] = d
        b_grad[:, at] += jnp.sum(d.astype(F32), axis=0, keepdims=True)
        o = dot_nn(m, w_out[at, :])
        g = dot_nt(d, w_in[:, at])
        out_sum = o if out_sum is None else out_sum + o
        back_sum = g if back_sum is None else back_sum + g
    pdn[...] = back_sum.astype(BF16)

    @pl.when(i < half)
    def _():
        part_own[...] = out_sum.astype(BF16)

    @pl.when(i >= half)
    def _():
        part_par[...] = out_sum.astype(BF16)


def cross_bwd_kernel(rows, length, heads, half, pick, h2, part, recv, eo, ep, gains, wo, c2, p, kv, wq,
                     dh2, e2, dc2, dkv, pdn, sums, dk_acc, dv_acc):
    i = pl.program_id(0)
    width = heads * HEAD

    @pl.when(i == 0)
    def _():
        sums[...] = jnp.zeros_like(sums)
        dk_acc[...] = jnp.zeros_like(dk_acc)
        dv_acc[...] = jnp.zeros_like(dv_acc)

    dn = part[...].astype(F32) + recv[...].astype(F32)
    y, rs = norm_parts(h2[...])
    g3 = jnp.where(i < half, eo[...].astype(F32), ep[...].astype(F32))
    d = g3 + norm_back(dn, y, rs, gains[2:3, :].astype(F32))
    dh2[...] = d
    e = d.astype(BF16)
    e2[...] = e

    @pl.when(i < half)
    def _():
        sums[0:1, :] += jnp.sum(dn * y, axis=0, keepdims=True)
        sums[1:2, :] += jnp.sum(dn, axis=0, keepdims=True)
        sums[2:3, :] += jnp.sum(d, axis=0, keepdims=True)
        sums[3:4, :] += jnp.sum(g3, axis=0, keepdims=True)

    da = dot_nt(e, wo[...]).astype(BF16).astype(F32)
    cf = c2[...].astype(F32)
    outs = []
    for r in range(rows):
        at = slice(r * length, (r + 1) * length)
        im = pick[i * rows + r]
        kr = kv[im, :, 0:width]
        vr = kv[im, :, width : 2 * width]
        pr = p[r]
        wide_o = spread_heads(da[at], heads)
        dpt = dot_nt(vr, wide_o)
        dv_acc[im] += dot_nn(pr, wide_o)
        pf = pr.astype(F32)
        ds = (pf * (dpt - jnp.sum(pf * dpt, axis=0, keepdims=True))).astype(BF16)
        outs.append(join_heads(dot_tn(ds, kr), length, heads))
        dk_acc[im] += dot_nn(ds, spread_heads(cf[at], heads)) * SCALE
    dc = (jnp.concatenate(outs, axis=0) * SCALE).astype(BF16)
    dc2[...] = dc
    pdn[...] = dot_nt(dc, wq[...]).astype(BF16)

    @pl.when(i == pl.num_programs(0) - 1)
    def _():
        dkv[:, :, 0:width] = dk_acc[...].astype(BF16)
        dkv[:, :, width : 2 * width] = dv_acc[...].astype(BF16)


def self_bwd_kernel(rows, length, heads, half, h1, dh2, part, recv, gains, wo, q, k, v, p, w,
                    dh1, e1, dq, dk, dv, part_own, part_par, sums, sums_in):
    i = pl.program_id(0)

    @pl.when(i == 0)
    def _():
        sums[...] = jnp.zeros_like(sums)
        sums_in[...] = jnp.zeros_like(sums_in)

    dn = part[...].astype(F32) + recv[...].astype(F32)
    y, rs = norm_parts(h1[...])
    d = dh2[...] + norm_back(dn, y, rs, gains[1:2, :].astype(F32))
    e = d.astype(BF16)
    e1[...] = e

    @pl.when(i < half)
    def _():
        dh1[...] = d
        sums[0:1, :] += jnp.sum(dn * y, axis=0, keepdims=True)
        sums[1:2, :] += jnp.sum(dn, axis=0, keepdims=True)
        sums[2:3, :] += jnp.sum(d, axis=0, keepdims=True)

    da = dot_nt(e, wo[...]).astype(BF16).astype(F32)
    qf, kf, vf = q[...].astype(F32), k[...].astype(F32), v[...].astype(F32)
    oq, ok, ov = [], [], []
    for r in range(rows):
        at = slice(r * length, (r + 1) * length)
        kr = kf[at].astype(BF16)
        vr = vf[at].astype(BF16)
        pr = p[r]
        wide_o = spread_heads(da[at], heads)
        dpt = dot_nt(vr, wide_o)
        ov.append(dot_nn(pr, wide_o))
        pf = pr.astype(F32)
        ds = (pf * (dpt - jnp.sum(pf * dpt, axis=0, keepdims=True))).astype(BF16)
        oq.append(join_heads(dot_tn(ds, kr), length, heads))
        ok.append(dot_nn(ds, spread_heads(qf[at], heads)))
    dqv = (jnp.concatenate(oq, axis=0) * SCALE).astype(BF16)
    dkv = (jnp.concatenate(ok, axis=0) * SCALE).astype(BF16)
    dvv = jnp.concatenate(ov, axis=0).astype(BF16)
    dq[...] = dqv
    dk[...] = dkv
    dv[...] = dvv
    sums_in[0:1, :] += jnp.sum(dqv.astype(F32), axis=0, keepdims=True)
    sums_in[1:2, :] += jnp.sum(dvv.astype(F32), axis=0, keepdims=True)
    back = (dot_nt(dqv, w[0]) + dot_nt(dkv, w[1]) + dot_nt(dvv, w[2])).astype(BF16)

    @pl.when(i < half)
    def _():
        part_own[...] = back

    @pl.when(i >= half)
    def _():
        part_par[...] = back


def text_bwd_kernel(x, dh1, part, recv, gains, out, sums):
    i = pl.program_id(0)

    @pl.when(i == 0)
    def _():
        sums[...] = jnp.zeros_like(sums)

    dn = part[...].astype(F32) + recv[...].astype(F32)
    y, rs = norm_parts(x[...].astype(F32))
    out[...] = dh1[...] + norm_back(dn, y, rs, gains[0:1, :].astype(F32))
    sums[0:1, :] += jnp.sum(dn * y, axis=0, keepdims=True)
    sums[1:2, :] += jnp.sum(dn, axis=0, keepdims=True)


def whole(shape):
    zeros = (0,) * len(shape)
    return pl.BlockSpec(shape, lambda i, *_: zeros)


def call(kernel, name, grid, ins, outs, args, scratch=(), prefetch=0, flops=0, exps=0):
    moved = sum(a.size * a.dtype.itemsize for a in args) + sum(
        functools.reduce(lambda u, v: u * v, s.shape, 1) * s.dtype.itemsize for s, _ in outs
    )
    return pl.pallas_call(
        kernel,
        out_shape=[s for s, _ in outs],
        grid_spec=pltpu.PrefetchScalarGridSpec(
            num_scalar_prefetch=prefetch,
            grid=grid,
            in_specs=list(ins),
            out_specs=[b for _, b in outs],
            scratch_shapes=list(scratch),
        ),
        compiler_params=pltpu.CompilerParams(vmem_limit_bytes=VMEM_BYTES),
        cost_estimate=pl.CostEstimate(flops=flops, transcendentals=exps, bytes_accessed=moved),
        name=name,
    )(*args)


def local(n_dp, orders, text, patches, segment_ids, image_of_row, gains, shifts, self_qkv, in_bias, self_out,
          cross_q, cross_kv, cross_out, ffn_in, ffn_in_bias, ffn_out, out_bias, cotangent):
    core = lax.axis_index("tensor")
    dp = lax.axis_index("dp")
    own, width = text.shape
    tokens = 2 * own
    rows, length = segment_ids.shape
    local_width = self_out.shape[0]
    heads = local_width // HEAD
    images, spots, half_dv = patches.shape
    hidden = ffn_in.shape[1]
    block_rows = 6 if (rows // 2) % 6 == 0 else 1
    block = block_rows * length
    steps = tokens // block
    half = steps // 2
    sd = jax.ShapeDtypeStruct

    swap = lambda v: lax.ppermute(v, "tensor", [(0, 1), (1, 0)])
    text_par = swap(text)
    cot_par = swap(cotangent)
    patches_par = swap(patches)

    w3 = jnp.transpose(self_qkv, (1, 0, 2))
    wkv = cross_kv.reshape(cross_kv.shape[0], 2 * local_width)
    flip = lambda v: jnp.where(core == 0, v, jnp.roll(v, rows // 2, axis=0))
    seg = flip(segment_ids)
    pick = flip(image_of_row)
    segk = seg[:, :, None]
    segq = jnp.tile(seg, (1, heads))[:, None, :]

    tok = lambda n: pl.BlockSpec((block, n), lambda i, *_: (i, 0))
    tok_other = lambda n: pl.BlockSpec((block, n), lambda i, *_: ((i + half) % steps, 0))
    tok_own = lambda n: pl.BlockSpec((block, n), lambda i, *_: (jnp.minimum(i, half - 1), 0))
    tok_par = lambda n: pl.BlockSpec((block, n), lambda i, *_: (jnp.maximum(i - half, 0), 0))
    row3 = lambda a, b: pl.BlockSpec((block_rows, a, b), lambda i, *_: (i, 0, 0))
    act = lambda n, dt=BF16: (sd((tokens, n), dt), tok(n))
    ql = heads * length
    sizes = (block_rows, length, heads, half)

    n1, q, k, v, p1, a1, part1 = call(
        functools.partial(self_fwd_kernel, *sizes), "self_fwd", (steps,),
        [tok_own(width), tok_par(width), whole(gains.shape), whole(shifts.shape), whole(w3.shape),
         whole(in_bias.shape), whole(self_out.shape), row3(length, 1), row3(1, ql)],
        [act(width), act(local_width), act(local_width), act(local_width),
         (sd((rows, length, ql), BF16), row3(length, ql)), act(local_width), act(width)],
        (text, text_par, gains, shifts, w3, in_bias, self_out, segk, segq),
        flops=2 * tokens * width * 4 * local_width, exps=rows * length * ql)
    recv1 = swap(part1)

    kv_bias = jnp.concatenate([jnp.zeros((local_width,), F32), in_bias[3].astype(F32)])[None, :]
    place = jnp.full((1,), core, jnp.int32)
    (kv,) = call(
        project_kernel, "project", (images,),
        [pl.BlockSpec((1, spots, half_dv), lambda i, *_: (i, 0, 0)),
         pl.BlockSpec((1, spots, half_dv), lambda i, *_: (i, 0, 0)),
         pl.BlockSpec((half_dv, 2 * local_width), lambda i, c: (c[0], 0)),
         pl.BlockSpec((half_dv, 2 * local_width), lambda i, c: (1 - c[0], 0)),
         whole(kv_bias.shape)],
        [(sd((images, spots, 2 * local_width), BF16),
          pl.BlockSpec((1, spots, 2 * local_width), lambda i, *_: (i, 0, 0)))],
        (place, patches, patches_par, wkv, wkv, kv_bias), prefetch=1,
        flops=4 * images * spots * 2 * half_dv * local_width)

    h1, n2, c2, p2, a2, part2 = call(
        functools.partial(cross_fwd_kernel, *sizes), "cross_fwd", (steps,),
        [tok_own(width), tok_par(width), tok(width), tok_other(width), whole(gains.shape), whole(shifts.shape),
         whole(in_bias.shape), whole(out_bias.shape), whole(cross_q.shape), whole(kv.shape), whole(cross_out.shape)],
        [act(width, F32), act(width), act(local_width), (sd((rows, spots, ql), BF16), row3(spots, ql)),
         act(local_width), act(width)],
        (pick, text, text_par, part1, recv1, gains, shifts, in_bias, out_bias, cross_q, kv, cross_out), prefetch=1,
        flops=2 * tokens * width * 2 * local_width + 4 * rows * ql * spots * local_width, exps=rows * ql * spots)
    recv2 = swap(part2)

    own_spec = lambda n: (sd((own, n), BF16), tok_own(n))
    par_spec = lambda n: (sd((own, n), BF16), tok_par(n))
    b_in = ffn_in_bias[None, :]
    h2, n3, m3, du3, e3, part3_own, part3_par, pdn3, ffn_in_bias_grad = call(
        functools.partial(ffn_kernel, half, 512 if hidden % 512 == 0 else hidden), "ffn", (steps,),
        [tok(width), tok(width), tok_other(width), tok_own(width), tok_par(width), whole(gains.shape),
         whole(shifts.shape), whole(out_bias.shape), whole(ffn_in.shape), whole(b_in.shape), whole(ffn_out.shape)],
        [act(width, F32), act(width), act(hidden), act(hidden), act(width), own_spec(width), par_spec(width),
         act(width), (sd((1, hidden), F32), whole((1, hidden)))],
        (h1, part2, recv2, cotangent, cot_par, gains, shifts, out_bias, ffn_in, b_in, ffn_out),
        flops=8 * tokens * width * hidden, exps=2 * tokens * hidden)
    recv3 = swap(pdn3)
    recv_out = swap(part3_par)
    layer_out = h2[:own] + (part3_own.astype(F32) + recv_out.astype(F32)) + out_bias[2].astype(F32)

    g_ffn_out = dot_tn(m3, e3).astype(BF16)
    g_ffn_in = dot_tn(n3, du3).astype(BF16)

    dh2, e2, dc2, dkv, pdn2, sums2 = call(
        functools.partial(cross_bwd_kernel, *sizes), "cross_bwd", (steps,),
        [tok(width), tok(width), tok_other(width), tok_own(width), tok_par(width), whole(gains.shape),
         whole(cross_out.shape), tok(local_width), row3(spots, ql), whole(kv.shape), whole(cross_q.shape)],
        [act(width, F32), act(width), act(local_width), (sd(kv.shape, BF16), whole(kv.shape)), act(width),
         (sd((8, width), F32), whole((8, width)))],
        (pick, h2, pdn3, recv3, cotangent, cot_par, gains, cross_out, c2, p2, kv, cross_q), prefetch=1,
        scratch=[pltpu.VMEM((images, spots, local_width), F32)] * 2,
        flops=2 * tokens * width * 2 * local_width + 8 * rows * ql * spots * local_width)
    recv_dn2 = swap(pdn2)

    g_cross_out = dot_tn(a2, e2).astype(BF16)
    g_cross_q = dot_tn(n2, dc2).astype(BF16)
    contract_images = lambda a: lax.dot_general(
        a, dkv, (((0, 1), (0, 1)), ((), ())), preferred_element_type=F32).astype(BF16)
    g_kv_own = contract_images(patches)
    g_kv_par = contract_images(patches_par)
    w_own = lax.dynamic_slice_in_dim(wkv, core * half_dv, half_dv, axis=0)
    w_par = lax.dynamic_slice_in_dim(wkv, (1 - core) * half_dv, half_dv, axis=0)
    terms = lambda w: lax.dot_general(dkv, w, (((2,), (1,)), ((), ())), preferred_element_type=F32)
    patch_grad = terms(w_own) + swap(terms(w_par).astype(BF16)).astype(F32)
    cross_q_bias = jnp.sum(dc2.astype(F32), axis=0)
    cross_v_bias = jnp.sum(dkv[:, :, local_width:].astype(F32), axis=(0, 1))

    dh1, e1, dq, dk, dv, part1_own, part1_par, sums1, sums_in = call(
        functools.partial(self_bwd_kernel, *sizes), "self_bwd", (steps,),
        [tok(width), tok(width), tok(width), tok_other(width), whole(gains.shape), whole(self_out.shape),
         tok(local_width), tok(local_width), tok(local_width), row3(length, ql), whole(w3.shape)],
        [(sd((own, width), F32), tok_own(width)), act(width), act(local_width), act(local_width), act(local_width),
         own_spec(width), par_spec(width), (sd((8, width), F32), whole((8, width))),
         (sd((8, local_width), F32), whole((8, local_width)))],
        (h1, dh2, pdn2, recv_dn2, gains, self_out, q, k, v, p1, w3),
        flops=2 * tokens * width * 4 * local_width)
    recv_dn1 = swap(part1_par)

    g_self_out = dot_tn(a1, e1).astype(BF16)
    g_qkv = jnp.stack([dot_tn(n1, d).astype(BF16) for d in (dq, dk, dv)])

    half_block = pl.BlockSpec((block, width), lambda i, *_: (i, 0))
    text_grad, sums0 = call(
        text_bwd_kernel, "text_bwd", (half,),
        [half_block, half_block, half_block, half_block, whole(gains.shape)],
        [(sd((own, width), F32), half_block), (sd((8, width), F32), whole((8, width)))],
        (text, dh1, part1_own, recv_dn1, gains))

    def all_reduce(value):
        rows_here = value.shape[0]
        mine = []
        for bit_a, bit_b in orders:
            perm = [(d * 2 + t, (d ^ (1 << (bit_a, bit_b)[t])) * 2 + t) for d in range(n_dp) for t in range(2)]
            bit = jnp.where(core == 0, dp >> bit_a, dp >> bit_b) & 1
            mine.append((perm, bit))
            rows_here //= 2
            send = lax.dynamic_slice_in_dim(value, (1 - bit) * rows_here, rows_here, axis=0)
            keep = lax.dynamic_slice_in_dim(value, bit * rows_here, rows_here, axis=0)
            got = lax.ppermute(send, ("dp", "tensor"), perm)
            value = (keep.astype(F32) + got.astype(F32)).astype(BF16)
        for perm, bit in reversed(mine):
            got = lax.ppermute(value, ("dp", "tensor"), perm)
            value = jnp.concatenate(
                [jnp.where(bit == 0, value, got), jnp.where(bit == 0, got, value)], axis=0)
        return value.astype(F32)

    def small_reduce(value, with_tensor):
        for bit, _ in orders:
            perm = [(d, d ^ (1 << bit)) for d in range(n_dp)]
            value = value + lax.ppermute(value, "dp", perm)
        return value + swap(value) if with_tensor else value

    ffn_out_grad = all_reduce(g_ffn_out)
    wide = hidden // 2
    r_in = all_reduce(jnp.concatenate([g_ffn_in[:, :wide], g_ffn_in[:, wide:]], axis=0))
    ffn_in_grad = jnp.concatenate([r_in[:width], r_in[width:]], axis=1)
    fold = lambda g: jnp.concatenate([g[: g.shape[0] // 2], g[g.shape[0] // 2 :]], axis=1)
    unfold = lambda g: jnp.concatenate([g[:, : g.shape[1] // 2], g[:, g.shape[1] // 2 :]], axis=0)
    r_cross = all_reduce(jnp.concatenate([g_cross_out, fold(g_cross_q), g_kv_own, g_kv_par], axis=0))
    cross_out_grad = r_cross[:local_width]
    cross_q_grad = unfold(r_cross[local_width : local_width + width // 2])
    base = local_width + width // 2
    kv_a, kv_b = r_cross[base : base + half_dv], r_cross[base + half_dv :]
    cross_kv_grad = jnp.concatenate(
        [jnp.where(core == 0, kv_a, kv_b), jnp.where(core == 0, kv_b, kv_a)], axis=0
    ).reshape(cross_kv.shape)
    r_self = all_reduce(jnp.concatenate([g_self_out, fold(g_qkv[0]), fold(g_qkv[1]), fold(g_qkv[2])], axis=0))
    self_out_grad = r_self[:local_width]
    hw = width // 2
    self_qkv_grad = jnp.stack(
        [unfold(r_self[local_width + j * hw : local_width + (j + 1) * hw]) for j in range(3)], axis=1)

    wide_sums = small_reduce(jnp.concatenate([sums0[0:2], sums1[0:3], sums2[0:4]], axis=0), True)
    gains_grad = jnp.stack([wide_sums[0], wide_sums[2], wide_sums[5]])
    shifts_grad = jnp.stack([wide_sums[1], wide_sums[3], wide_sums[6]])
    out_bias_grad = jnp.stack([wide_sums[4], wide_sums[7], wide_sums[8]])
    narrow = small_reduce(jnp.concatenate(
        [sums_in[0], sums_in[1], cross_q_bias, cross_v_bias, ffn_in_bias_grad[0]]), False)
    in_bias_grad = narrow[: 4 * local_width].reshape(4, local_width)
    ffn_in_bias_grad = narrow[4 * local_width :]

    return (layer_out, text_grad, patch_grad, gains_grad, shifts_grad, self_qkv_grad, in_bias_grad, self_out_grad,
            cross_q_grad, cross_kv_grad, cross_out_grad, ffn_in_grad, ffn_in_bias_grad, ffn_out_grad, out_bias_grad)


def bit_orders(mesh):
    n_dp = mesh.shape["dp"]
    bits = max(n_dp.bit_length() - 1, 0)
    third = (bits + 1) // 4 if bits else 0
    x_bits = list(range(0, third))
    y_bits = list(range(third, 2 * third))
    z_bits = list(range(2 * third, bits))
    return list(zip(x_bits + y_bits + z_bits, y_bits + x_bits + z_bits))


def solution(mesh):
    both = P(("dp", "tensor"), None)
    in_specs = (both, P("dp", None, "tensor"), P("dp", None), P("dp"), P(), P(), P(None, None, "tensor"),
                P(None, "tensor"), P("tensor", None), P(None, "tensor"), P(None, None, "tensor"), P("tensor", None),
                P(None, "tensor"), P("tensor"), P("tensor", None), P(), both)
    out_specs = (both, both, P("dp", None, "tensor"), P(), P(), P(None, None, "tensor"), P(None, "tensor"),
                 P("tensor", None), P(None, "tensor"), P(None, None, "tensor"), P("tensor", None), P(None, "tensor"),
                 P("tensor"), P("tensor", None), P())
    fn = functools.partial(local, mesh.shape["dp"], bit_orders(mesh))
    return jax.shard_map(fn, mesh=mesh, in_specs=in_specs, out_specs=out_specs, check_vma=False)
```

time: 1190 us -> 442 us (0.37)
  waiting for transfers between devices: 537 us -> 146 us
  matrix products: 209 us -> 31.5 us
  local copies, waits for them, and re-layouts: 188 us -> 28.7 us
  blocking collectives: 123 us -> 0 us
  Pallas kernels: 0 us -> 108 us
  starting transfers between devices: 11.4 us -> 59.4 us
  other arithmetic: 90.7 us -> 58.9 us
  between operations: 15.9 us -> 2.12 us
    psum x1 -> x0, waiting for transfers between devices: 393 us -> none  [local(): lax.psum((self_qkv_grad, in_bias_grad, self_out_grad, cross_q_grad, cross...]
    dot_general x48 -> x12, matrix products: 209 us -> 31.5 us  [the longest x8 16.3 us: dot_tn(): lax.dot_general(a, b, (((0,), (0,)), ((), ())), preferred_element_type=F32)]
    ppermute x0 -> x51, waiting for transfers between devices: none -> 146 us  [the longest x16 62.5 us: all_reduce(): got = lax.ppermute(send, ('dp', 'tensor'), perm)]
    psum x2 -> x0, blocking collectives: 123 us -> none  [the longest x1 81.8 us: local(): lax.psum((self_qkv_grad, in_bias_grad, self_out_grad, cross_q_grad, cross...]
    pallas_call x0 -> x7, Pallas kernels: none -> 108 us  [call(): pl.pallas_call(kernel, out_shape=[s for s, _ in outs], grid_spec=pltpu.Pr...]
    convert_element_type x24 -> x0, local copies, waits for them, and re-layouts: 73.4 us -> none  [the longest x8 20.3 us: attend(): mixed.reshape(-1, mixed.shape[2] * mixed.shape[3]).astype(jnp.bfloat16)]
    all_gather x11 -> x0, waiting for transfers between devices: 71.6 us -> none  [the longest x9 48.1 us: gather_rows(): return lax.all_gather(local_rows, 'tensor', axis=0, tiled=True)]
    reduce_scatter x9 -> x0, waiting for transfers between devices: 70.5 us -> none  [the longest x8 70.4 us: reduce_rows(): lax.psum_scatter(lax.dot_general(piece, right, (((1,), (axis_right,)), ((...]
  transfers between devices with their start and end apart: 21 -> 51, of which waited for: 16 -> 27; matrix products, arithmetic and copies ran while one was open for 18% -> 24% of each run, Pallas kernels for 0% -> 17%
where the time goes in v1:
time: 442 us; the launch traced here: 435 us
  waiting for transfers between devices  146 us (33%)
  Pallas kernels  108 us (24%)
  starting transfers between devices  59.4 us (13%)
  other arithmetic  58.9 us (13%)
  matrix products  31.5 us (7%)
  local copies, waits for them, and re-layouts  28.7 us (6%)
    pallas_call x7, Pallas kernels, call(): pl.pallas_call(kernel, out_shape=[s for s, _ in outs], grid_spec=pltpu.Pr...  108 us
    ppermute x16, waiting for transfers between devices, all_reduce(): got = lax.ppermute(send, ('dp', 'tensor'), perm)  62.5 us
    ppermute x16, waiting for transfers between devices, all_reduce(): got = lax.ppermute(value, ('dp', 'tensor'), perm)  50.2 us
    ppermute x8, waiting for transfers between devices, small_reduce(): value = value + lax.ppermute(value, 'dp', perm)  29.6 us
    ppermute x16, starting transfers between devices, all_reduce(): got = lax.ppermute(send, ('dp', 'tensor'), perm)  26.9 us
    ppermute x16, starting transfers between devices, all_reduce(): got = lax.ppermute(value, ('dp', 'tensor'), perm)  18.7 us
    dot_general x8, matrix products, dot_tn(): lax.dot_general(a, b, (((0,), (0,)), ((), ())), preferred_element_type=F32)  16.3 us
    concatenate x1, other arithmetic, local(): jnp.concatenate([g_self_out, fold(g_qkv[0]), fold(g_qkv[1]), fold(g_qkv[2...  12.2 us
  transfers between devices with their start and end apart: 51, of which 27 were waited for; matrix products, arithmetic and copies ran while one was open for 24% of the time, Pallas kernels for 17%

profile of v1, /device:TPU:0, one launch (start us, length us, event | category | flops | bytes accessed | tf_op | source)
XLA Modules:
  0.0 434.5 jit_solution(2513429908317578651)
XLA Ops:
  5.4 15.6 %self_fwd.1 = (bf16[960,768]{1,0:T(8,128)(2,1)}, bf16[960,384]{1,0:T(8,128)(2,1)}, bf16[960,384]{1,0:T(8,128)(2,1)}, bf16[960,384]{1,0:T(8,128)(2,1)}, bf16[24,4...) custom-call(bf16[480,768]{1,0:T(8,128)(2,1)} %x.3, bf16[480,768]{1,0:T(8,128)(2,1)} %copy-done.35, ...), custom_call_target="tpu_custom_call" | custom-call | flops 2264924160 | bytes 10232064 | tf_op jit(solution)/shard_map/self_fwd/pallas_call | solution.py:300
  25.1 11.0 %project.1.kv = bf16[12,145,768]{2,1,0:T(8,128)(2,1)} custom-call(s32[1]{0:T(128)} %bitcast.2.place, bf16[12,145,512]{2,1,0:T(8,128)(2,1)} %po.1, bf16[12,145,512]{2,1,0:T(8,128)(2,1)} %copy-done.31, bf16[1024,768]{1,0:T(8,128)(2,1)} %bitcast.54, bf16[1024,768]{1,0:T(8,128)(2,1)} %bitcast.55, f32[1,768]{1,0:T(1,128)} %reshape.55.bias), custom_call_target="tpu_custom_call" | custom-call | flops 2736783360 | bytes 9384964 | tf_op jit(solution)/shard_map/project/pallas_call | solution.py:300
  36.1 13.1 %cross_fwd.1 = (f32[960,768]{1,0:T(8,128)}, bf16[960,768]{1,0:T(8,128)(2,1)}, bf16[960,384]{1,0:T(8,128)(2,1)}, bf16[24,145,240]{2,1,0:T(8,128)(2,1)}, bf16[960,...) custom-call(s32[24]{0:T(128)} %broadcast_select_fusion.32.pick, bf16[480,768]{1,0:T(8,128)(2,1)} %x.3, ...), custom_call_target="tpu_custom_call" | custom-call | flops 2415329280 | bytes 17336160 | tf_op jit(solution)/shard_map/cross_fwd/pallas_call | solution.py:300
  55.4 18.9 %ffn.1 = (f32[960,768]{1,0:T(8,128)}, bf16[960,768]{1,0:T(8,128)(2,1)}, bf16[960,1536]{1,0:T(8,128)(2,1)}, bf16[960,1536]{1,0:T(8,128)(2,1)}, bf16[960,768]{1,0:...) custom-call(f32[960,768]{1,0:T(8,128)} %get-tuple-element.55.h1, ...), custom_call_target="tpu_custom_call" | custom-call | flops 9059696640 | bytes 26860032 | tf_op jit(solution)/shard_map/ffn/pallas_call | solution.py:300
  74.7 4.9 %convolution_convert_fusion.1 = bf16[768,1536]{1,0:T(8,128)(2,1)S(1)} fusion(bf16[960,768]{1,0:T(8,128)(2,1)} %get-tuple-element.89, bf16[960,1536]{1,0:T(8,128)(2,1)} %get-tuple-element.90), kind=kOutput, calls=%fused_computation.4 | convolution fusion | flops 2266103808 | bytes 6782976 | tf_op jit(solution)/shard_map/dot_general | solution.py:28
  104.7 12.9 %collective-permute-done.43 = bf16[768,768]{1,0:T(8,128)(2,1)} collective-permute-done((bf16[768,768]{1,0:T(8,128)(2,1)}, bf16[768,768]{1,0:T(8,128)(2,1)}, u32[]{:S(2)}, u32[]{:S(2)}) %collective-permute-start.43) | collective-permute-done | bytes 1179680 | tf_op jit(solution)/shard_map/ppermute | solution.py:462
  122.2 24.0 %cross_bwd.1 = (f32[960,768]{1,0:T(8,128)}, bf16[960,768]{1,0:T(8,128)(2,1)}, bf16[960,384]{1,0:T(8,128)(2,1)}, bf16[12,145,768]{2,1,0:T(8,128)(2,1)}, bf16[960,768]{1,0:T(8,128)(2,1)}, /*index=5*/f32[8,768]{1,0:T(8,128)}) custom-call(s32[24]{0:T(128)} %broadcast_select_fusion.32.pick, f32[960,768]{1,0:T(8,128)} %get-tuple-element.57.h2, ...), custom_call_target="tpu_custom_call" | custom-call | flops 3698196480 | bytes 22970208 | tf_op jit(solution)/shard_map/cross_bwd/pallas_call | solution.py:300
  146.4 5.2 %fusion = bf16[512,768]{1,0:T(8,128)(2,1)} fusion(bf16[12,145,768]{2,1,0:T(8,128)(2,1)} %get-tuple-element.73, bf16[12,145,512]{2,1,0:T(8,128)(2,1)} %po.1), kind=kOutput, calls=%fused_computation.36 | convolution fusion | flops 1368784896 | bytes 5240832 | tf_op jit(solution)/shard_map/dot_general | solution.py:420
  169.1 8.1 %collective-permute-done.37 = bf16[192,768]{1,0:T(8,128)(2,1)S(1)} collective-permute-done((bf16[192,768]{1,0:T(8,128)(2,1)S(1)}, bf16[192,768]{1,0:T(8,128)(2,1)S(1)}, u32[]{:S(2)}, u32[]{:S(2)}) %collective-permute-start.37) | collective-permute-done | bytes 294944 | tf_op jit(solution)/shard_map/ppermute | solution.py:462
  184.1 7.3 %collective-permute-done.38 = bf16[96,768]{1,0:T(8,128)(2,1)S(1)} collective-permute-done((bf16[96,768]{1,0:T(8,128)(2,1)S(1)}, bf16[96,768]{1,0:T(8,128)(2,1)S(1)}, u32[]{:S(2)}, u32[]{:S(2)}) %collective-permute-start.38) | collective-permute-done | bytes 147488 | tf_op jit(solution)/shard_map/ppermute | solution.py:462
  194.7 7.1 %collective-permute-done.39 = bf16[96,768]{1,0:T(8,128)(2,1)S(1)} collective-permute-done((bf16[96,768]{1,0:T(8,128)(2,1)S(1)}, bf16[96,768]{1,0:T(8,128)(2,1)S(1)}, u32[]{:S(2)}, u32[]{:S(2)}) %collective-permute-start.39) | collective-permute-done | bytes 147488 | tf_op jit(solution)/shard_map/ppermute | solution.py:465
  222.1 21.4 %self_bwd.1 = (f32[480,768]{1,0:T(8,128)}, bf16[960,768]{1,0:T(8,128)(2,1)}, bf16[960,384]{1,0:T(8,128)(2,1)}, bf16[960,384]{1,0:T(8,128)(2,1)}, bf16[960,384]{1...) custom-call(f32[960,768]{1,0:T(8,128)} %get-tuple-element.55.h1, ...), custom_call_target="tpu_custom_call" | custom-call | flops 2264924160 | bytes 20556288 | tf_op jit(solution)/shard_map/self_bwd/pallas_call | solution.py:300
  256.5 12.2 %maximum_maximum_fusion = bf16[1536,768]{1,0:T(8,128)(2,1)S(1)} fusion(bf16[384,384]{1,0:T(8,128)(2,1)S(1)} %get-tuple-element.141, bf16[384,384]{1,0:T(8,128)(2,1)S(1)} %get-tuple-element.140, bf16[384,384]{1,0:T(8,128)(2,1)S(1)} %get-tuple-element.165, bf16[384,384]{1,0:T(8,128)(2,1)S(1)} %get-tuple-element.166, ...), kind=kLoop, calls=%fused_computation.13 | loop fusion | flops 16515072 | bytes 4718592 | tf_op jit(solution)/shard_map/concatenate | solution.py:490
  289.1 18.9 %collective-permute-done.10 = f32[9,768]{1,0:T(8,128)S(1)} collective-permute-done((f32[9,768]{1,0:T(8,128)S(1)}, f32[9,768]{1,0:T(8,128)S(1)}, u32[]{:S(2)}, u32[]{:S(2)}) %collective-permute-start.10) | collective-permute-done | bytes 27680 | tf_op jit(solution)/shard_map/ppermute | solution.py:473
  324.9 5.1 %convert_add_fusion = f32[12,145,512]{2,1,0:T(8,128)} fusion(bf16[12,145,512]{2,1,0:T(8,128)(2,1)} %collective-permute-done.9, bf16[12,145,768]{2,1,0:T(8,128)(2,1)S(1)} %copy-done.20, bf16[1024,768]{1,0:T(8,128)(2,1)S(1)} %bitcast.57, s32[]{:T(128)S(6)} %select_n.283), kind=kOutput, calls=%fused_computation.1 | convolution fusion | flops 1370173440 | bytes 8933380 | tf_op jit(solution)/shard_map/dot_general | solution.py:426
  334.3 7.0 %collective-permute-done.30 = bf16[112,768]{1,0:T(8,128)(2,1)S(1)} collective-permute-done((bf16[112,768]{1,0:T(8,128)(2,1)S(1)}, bf16[112,768]{1,0:T(8,128)(2,1)S(1)}, u32[]{:S(2)}, u32[]{:S(2)}) %collective-permute-start.30) | collective-permute-done | bytes 172064 | tf_op jit(solution)/shard_map/ppermute | solution.py:462
  345.0 6.8 %collective-permute-done.31 = bf16[112,768]{1,0:T(8,128)(2,1)S(1)} collective-permute-done((bf16[112,768]{1,0:T(8,128)(2,1)S(1)}, bf16[112,768]{1,0:T(8,128)(2,1)S(1)}, u32[]{:S(2)}, u32[]{:S(2)}) %collective-permute-start.31) | collective-permute-done | bytes 172064 | tf_op jit(solution)/shard_map/ppermute | solution.py:465
  356.6 11.6 %collective-permute-done.17 = bf16[192,768]{1,0:T(8,128)(2,1)S(1)} collective-permute-done((bf16[192,768]{1,0:T(8,128)(2,1)S(1)}, bf16[192,768]{1,0:T(8,128)(2,1)S(1)}, u32[]{:S(2)}, u32[]{:S(2)}) %collective-permute-start.17) | collective-permute-done | bytes 294944 | tf_op jit(solution)/shard_map/ppermute | solution.py:462
  371.1 6.3 %collective-permute-done.18 = bf16[96,768]{1,0:T(8,128)(2,1)S(1)} collective-permute-done((bf16[96,768]{1,0:T(8,128)(2,1)S(1)}, bf16[96,768]{1,0:T(8,128)(2,1)S(1)}, u32[]{:S(2)}, u32[]{:S(2)}) %collective-permute-start.18) | collective-permute-done | bytes 147488 | tf_op jit(solution)/shard_map/ppermute | solution.py:462
  380.4 6.0 %collective-permute-done.19 = bf16[96,768]{1,0:T(8,128)(2,1)S(1)} collective-permute-done((bf16[96,768]{1,0:T(8,128)(2,1)S(1)}, bf16[96,768]{1,0:T(8,128)(2,1)S(1)}, u32[]{:S(2)}, u32[]{:S(2)}) %collective-permute-start.19) | collective-permute-done | bytes 147488 | tf_op jit(solution)/shard_map/ppermute | solution.py:465
  388.0 7.5 %collective-permute-done.20 = bf16[192,768]{1,0:T(8,128)(2,1)S(1)} collective-permute-done((bf16[192,768]{1,0:T(8,128)(2,1)S(1)}, bf16[192,768]{1,0:T(8,128)(2,1)S(1)}, u32[]{:S(2)}, u32[]{:S(2)}) %collective-permute-start.20) | collective-permute-done | bytes 294944 | tf_op jit(solution)/shard_map/ppermute | solution.py:465
  400.6 10.2 %collective-permute-done.21 = bf16[384,768]{1,0:T(8,128)(2,1)S(1)} collective-permute-done((bf16[384,768]{1,0:T(8,128)(2,1)S(1)}, bf16[384,768]{1,0:T(8,128)(2,1)S(1)}, u32[]{:S(2)}, u32[]{:S(2)}) %collective-permute-start.21) | collective-permute-done | bytes 589856 | tf_op jit(solution)/shard_map/ppermute | solution.py:465
  415.9 5.2 %reshape.54 = f32[1024,2,384]{2,1,0:T(2,128)} reshape(f32[1024,768]{1,0:T(8,128)} %pad_maximum_fusion.2) | data formatting | bytes 6291456 | tf_op jit(solution)/shard_map/reshape | solution.py:489
  423.3 5.4 %collective-permute-done.22 = bf16[768,768]{1,0:T(8,128)(2,1)} collective-permute-done((bf16[768,768]{1,0:T(8,128)(2,1)}, bf16[768,768]{1,0:T(8,128)(2,1)}, u32[]{:S(2)}, u32[]{:S(2)}) %collective-permute-start.22) | collective-permute-done | bytes 1179680 | tf_op jit(solution)/shard_map/ppermute | solution.py:465
  (311 shorter events, 180.7 us)
Async XLA Ops:
  1.2 22.7 %collective-permute-start.2 = (bf16[12,145,512]{2,1,0:T(8,128)(2,1)}, bf16[12,145,512]{2,1,0:T(8,128)(2,1)S(1)}, u32[]{:S(2)}, u32[]{:S(2)}) collective-permute-start(bf16[12,145,512]{2,1,0:T(8,128)(2,1)} %po.1), channel_id=1, source_target_pairs={{0,1},{1,0},{2,3},{3,2},{4,5},{5,4},{6,7},{7,6},{8,9},{9,8},{10,11... | collective-permute-start | bytes 5345288 | tf_op jit(solution)/shard_map/ppermute | solution.py:333
  21.0 15.2 %collective-permute-start.1 = (bf16[960,768]{1,0:T(8,128)(2,1)}, bf16[960,768]{1,0:T(8,128)(2,1)}, u32[]{:S(2)}, u32[]{:S(2)}) collective-permute-start(bf16[960,768]{1,0:T(8,128)(2,1)} %get-tuple-element.54.part), channel_id=1, source_target_pairs={{0,1},{1,0},{2,3},{3,2},{4,5},{5,4},{6,7},{7,6},{8,9},{9,8},{10,11... | collective-permute-start | bytes 4423688 | tf_op jit(solution)/shard_map/ppermute | solution.py:333
  74.3 17.4 %collective-permute-start.5 = (bf16[480,768]{1,0:T(8,128)(2,1)}, bf16[480,768]{1,0:T(8,128)(2,1)}, u32[]{:S(2)}, u32[]{:S(2)}) collective-permute-start(bf16[480,768]{1,0:T(8,128)(2,1)} %get-tuple-element.59), channel_id=1, source_target_pairs={{0,1},{1,0},{2,3},{3,2},{4,5},{5,4},{6,7},{7,6},{8,9},{9,8},{10,11... | collective-permute-start | bytes 2211848 | tf_op jit(solution)/shard_map/ppermute | solution.py:333
  81.5 17.3 %collective-permute-start.35 = (bf16[768,768]{1,0:T(8,128)(2,1)S(1)}, bf16[768,768]{1,0:T(8,128)(2,1)}, u32[]{:S(2)}, u32[]{:S(2)}) collective-permute-start(bf16[768,768]{1,0:T(8,128)(2,1)S(1)} %fusion.2), channel_id=1, source_target_pairs={{0,2},{1,5},{2,0},{3,7},{4,6},{5,1},{6,4},{7,3},{8,10},{9,13},{10,... | collective-permute-start | bytes 3538952 | tf_op jit(solution)/shard_map/ppermute | solution.py:462
  89.9 27.7 %collective-permute-start.43 = (bf16[768,768]{1,0:T(8,128)(2,1)}, bf16[768,768]{1,0:T(8,128)(2,1)}, u32[]{:S(2)}, u32[]{:S(2)}) collective-permute-start(bf16[768,768]{1,0:T(8,128)(2,1)} %constant_dynamic-slice_fusion.3), channel_id=1, source_target_pairs={{0,2},{1,5},{2,0},{3,7},{4,6},{5,1},{6,4},{7,3},{8,10},{9,13},{10,... | collective-permute-start | bytes 3538952 | tf_op jit(solution)/shard_map/ppermute | solution.py:462
  90.3 31.9 %collective-permute-start.6 = (bf16[960,768]{1,0:T(8,128)(2,1)}, bf16[960,768]{1,0:T(8,128)(2,1)}, u32[]{:S(2)}, u32[]{:S(2)}) collective-permute-start(bf16[960,768]{1,0:T(8,128)(2,1)} %get-tuple-element.60.part), channel_id=1, source_target_pairs={{0,1},{1,0},{2,3},{3,2},{4,5},{5,4},{6,7},{7,6},{8,9},{9,8},{10,11... | collective-permute-start | bytes 4423688 | tf_op jit(solution)/shard_map/ppermute | solution.py:333
  102.7 61.8 %collective-permute-start.36 = (bf16[384,768]{1,0:T(8,128)(2,1)}, bf16[384,768]{1,0:T(8,128)(2,1)}, u32[]{:S(2)}, u32[]{:S(2)}) collective-permute-start(bf16[384,768]{1,0:T(8,128)(2,1)} %constant_dynamic-slice_fusion.6), channel_id=1, source_target_pairs={{0,4},{1,3},{2,6},{3,1},{4,0},{5,7},{6,2},{7,5},{8,12},{9,11},{10,... | collective-permute-start | bytes 1769480 | tf_op jit(solution)/shard_map/ppermute | solution.py:462
  120.1 47.3 %collective-permute-start.44 = (bf16[384,768]{1,0:T(8,128)(2,1)}, bf16[384,768]{1,0:T(8,128)(2,1)}, u32[]{:S(2)}, u32[]{:S(2)}) collective-permute-start(bf16[384,768]{1,0:T(8,128)(2,1)} %constant_dynamic-slice_fusion.2), channel_id=1, source_target_pairs={{0,4},{1,3},{2,6},{3,1},{4,0},{5,7},{6,2},{7,5},{8,12},{9,11},{10,... | collective-permute-start | bytes 1769480 | tf_op jit(solution)/shard_map/ppermute | solution.py:462
  146.3 75.9 %collective-permute-start.7 = (bf16[960,768]{1,0:T(8,128)(2,1)}, bf16[960,768]{1,0:T(8,128)(2,1)}, u32[]{:S(2)}, u32[]{:S(2)}) collective-permute-start(bf16[960,768]{1,0:T(8,128)(2,1)} %get-tuple-element.64.part), channel_id=1, source_target_pairs={{0,1},{1,0},{2,3},{3,2},{4,5},{5,4},{6,7},{7,6},{8,9},{9,8},{10,11... | collective-permute-start | bytes 4423688 | tf_op jit(solution)/shard_map/ppermute | solution.py:333
  154.6 170.2 %collective-permute-start.9 = (bf16[12,145,512]{2,1,0:T(8,128)(2,1)}, bf16[12,145,512]{2,1,0:T(8,128)(2,1)}, u32[]{:S(2)}, u32[]{:S(2)}) collective-permute-start(bf16[12,145,512]{2,1,0:T(8,128)(2,1)} %convolution_convert_fusion.2), channel_id=1, source_target_pairs={{0,1},{1,0},{2,3},{3,2},{4,5},{5,4},{6,7},{7,6},{8,9},{9,8},{10,11... | collective-permute-start | bytes 5345288 | tf_op jit(solution)/shard_map/ppermute | solution.py:333
  162.7 57.1 %collective-permute-start.27 = (bf16[896,768]{1,0:T(8,128)(2,1)S(1)}, bf16[896,768]{1,0:T(8,128)(2,1)S(1)}, u32[]{:S(2)}, u32[]{:S(2)}) collective-permute-start(bf16[896,768]{1,0:T(8,128)(2,1)S(1)} %constant_dynamic-slice_fusion.10), channel_id=1, source_target_pairs={{0,2},{1,5},{2,0},{3,7},{4,6},{5,1},{6,4},{7,3},{8,10},{9,13},{10,... | collective-permute-start | bytes 4128776 | tf_op jit(solution)/shard_map/ppermute | solution.py:462
  211.9 65.1 %collective-permute-start.41 = (bf16[384,768]{1,0:T(8,128)(2,1)S(1)}, bf16[384,768]{1,0:T(8,128)(2,1)S(1)}, u32[]{:S(2)}, u32[]{:S(2)}) collective-permute-start(bf16[384,768]{1,0:T(8,128)(2,1)S(1)} %pad_maximum_fusion.16), channel_id=1, source_target_pairs={{0,4},{1,3},{2,6},{3,1},{4,0},{5,7},{6,2},{7,5},{8,12},{9,11},{10,... | collective-permute-start | bytes 1769480 | tf_op jit(solution)/shard_map/ppermute | solution.py:465
  217.0 70.1 %collective-permute-start.49 = (bf16[384,768]{1,0:T(8,128)(2,1)}, bf16[384,768]{1,0:T(8,128)(2,1)}, u32[]{:S(2)}, u32[]{:S(2)}) collective-permute-start(bf16[384,768]{1,0:T(8,128)(2,1)} %pad_maximum_fusion.17), channel_id=1, source_target_pairs={{0,4},{1,3},{2,6},{3,1},{4,0},{5,7},{6,2},{7,5},{8,12},{9,11},{10,... | collective-permute-start | bytes 1769480 | tf_op jit(solution)/shard_map/ppermute | solution.py:465
  243.5 37.2 %collective-permute-start.8 = (bf16[480,768]{1,0:T(8,128)(2,1)}, bf16[480,768]{1,0:T(8,128)(2,1)}, u32[]{:S(2)}, u32[]{:S(2)}) collective-permute-start(bf16[480,768]{1,0:T(8,128)(2,1)} %get-tuple-element.71), channel_id=1, source_target_pairs={{0,1},{1,0},{2,3},{3,2},{4,5},{5,4},{6,7},{7,6},{8,9},{9,8},{10,11... | collective-permute-start | bytes 2211848 | tf_op jit(solution)/shard_map/ppermute | solution.py:333
  273.4 40.2 %collective-permute-start.28 = (bf16[448,768]{1,0:T(8,128)(2,1)}, bf16[448,768]{1,0:T(8,128)(2,1)}, u32[]{:S(2)}, u32[]{:S(2)}) collective-permute-start(bf16[448,768]{1,0:T(8,128)(2,1)} %constant_dynamic-slice_fusion.9), channel_id=1, source_target_pairs={{0,4},{1,3},{2,6},{3,1},{4,0},{5,7},{6,2},{7,5},{8,12},{9,11},{10,... | collective-permute-start | bytes 2064392 | tf_op jit(solution)/shard_map/ppermute | solution.py:462
  277.8 63.6 %collective-permute-start.15 = (bf16[768,768]{1,0:T(8,128)(2,1)}, bf16[768,768]{1,0:T(8,128)(2,1)}, u32[]{:S(2)}, u32[]{:S(2)}) collective-permute-start(bf16[768,768]{1,0:T(8,128)(2,1)} %constant_dynamic-slice_fusion.14), channel_id=1, source_target_pairs={{0,2},{1,5},{2,0},{3,7},{4,6},{5,1},{6,4},{7,3},{8,10},{9,13},{10,... | collective-permute-start | bytes 3538952 | tf_op jit(solution)/shard_map/ppermute | solution.py:462
  280.7 71.2 %collective-permute-start.42 = (bf16[768,768]{1,0:T(8,128)(2,1)}, bf16[768,768]{1,0:T(8,128)(2,1)}, u32[]{:S(2)}, u32[]{:S(2)}) collective-permute-start(bf16[768,768]{1,0:T(8,128)(2,1)} %pad_maximum_fusion.7), channel_id=1, source_target_pairs={{0,2},{1,5},{2,0},{3,7},{4,6},{5,1},{6,4},{7,3},{8,10},{9,13},{10,... | collective-permute-start | bytes 3538952 | tf_op jit(solution)/shard_map/ppermute | solution.py:465
  287.1 20.8 %collective-permute-start.10 = (f32[9,768]{1,0:T(8,128)S(1)}, f32[9,768]{1,0:T(8,128)S(1)}, u32[]{:S(2)}, u32[]{:S(2)}) collective-permute-start(f32[9,768]{1,0:T(8,128)S(1)} %pad_maximum_fusion.22), channel_id=1, source_target_pairs={{0,2},{2,0},{4,6},{6,4},{8,10},{10,8},{12,14},{14,12},{16,18},{18,... | collective-permute-start | bytes 82952 | tf_op jit(solution)/shard_map/ppermute | solution.py:473
  312.1 85.4 %collective-permute-start.50 = (bf16[768,768]{1,0:T(8,128)(2,1)S(1)}, bf16[768,768]{1,0:T(8,128)(2,1)S(1)}, u32[]{:S(2)}, u32[]{:S(2)}) collective-permute-start(bf16[768,768]{1,0:T(8,128)(2,1)S(1)} %pad_maximum_fusion.8), channel_id=1, source_target_pairs={{0,2},{1,5},{2,0},{3,7},{4,6},{5,1},{6,4},{7,3},{8,10},{9,13},{10,... | collective-permute-start | bytes 3538952 | tf_op jit(solution)/shard_map/ppermute | solution.py:465
  351.9 17.1 %collective-permute-start.32 = (bf16[224,768]{1,0:T(8,128)(2,1)S(1)}, bf16[224,768]{1,0:T(8,128)(2,1)S(1)}, u32[]{:S(2)}, u32[]{:S(2)}) collective-permute-start(bf16[224,768]{1,0:T(8,128)(2,1)S(1)} %pad_maximum_fusion.18), channel_id=1, source_target_pairs={{0,8},{1,9},{2,10},{3,11},{4,12},{5,13},{6,14},{7,15},{8,0},{9,1},... | collective-permute-start | bytes 1032200 | tf_op jit(solution)/shard_map/ppermute | solution.py:465
  369.1 17.4 %collective-permute-start.33 = (bf16[448,768]{1,0:T(8,128)(2,1)S(1)}, bf16[448,768]{1,0:T(8,128)(2,1)S(1)}, u32[]{:S(2)}, u32[]{:S(2)}) collective-permute-start(bf16[448,768]{1,0:T(8,128)(2,1)S(1)} %pad_maximum_fusion.11), channel_id=1, source_target_pairs={{0,4},{1,3},{2,6},{3,1},{4,0},{5,7},{6,2},{7,5},{8,12},{9,11},{10,... | collective-permute-start | bytes 2064392 | tf_op jit(solution)/shard_map/ppermute | solution.py:465
  386.9 26.2 %collective-permute-start.34 = (bf16[896,768]{1,0:T(8,128)(2,1)S(1)}, bf16[896,768]{1,0:T(8,128)(2,1)S(1)}, u32[]{:S(2)}, u32[]{:S(2)}) collective-permute-start(bf16[896,768]{1,0:T(8,128)(2,1)S(1)} %pad_maximum_fusion.4), channel_id=1, source_target_pairs={{0,2},{1,5},{2,0},{3,7},{4,6},{5,1},{6,4},{7,3},{8,10},{9,13},{10,... | collective-permute-start | bytes 4128776 | tf_op jit(solution)/shard_map/ppermute | solution.py:465
  395.6 15.2 %collective-permute-start.21 = (bf16[384,768]{1,0:T(8,128)(2,1)S(1)}, bf16[384,768]{1,0:T(8,128)(2,1)S(1)}, u32[]{:S(2)}, u32[]{:S(2)}) collective-permute-start(bf16[384,768]{1,0:T(8,128)(2,1)S(1)} %pad_maximum_fusion.14), channel_id=1, source_target_pairs={{0,4},{1,3},{2,6},{3,1},{4,0},{5,7},{6,2},{7,5},{8,12},{9,11},{10,... | collective-permute-start | bytes 1769480 | tf_op jit(solution)/shard_map/ppermute | solution.py:465
  412.2 16.5 %collective-permute-start.22 = (bf16[768,768]{1,0:T(8,128)(2,1)}, bf16[768,768]{1,0:T(8,128)(2,1)}, u32[]{:S(2)}, u32[]{:S(2)}) collective-permute-start(bf16[768,768]{1,0:T(8,128)(2,1)} %pad_maximum_fusion.5), channel_id=1, source_target_pairs={{0,2},{1,5},{2,0},{3,7},{4,6},{5,1},{6,4},{7,3},{8,10},{9,13},{10,... | collective-permute-start | bytes 3538952 | tf_op jit(solution)/shard_map/ppermute | solution.py:465
  (70 other events, 484.8 us)
